TPU v7x, 32 devices: a whole 2x2x4 slice. The times are simulated.
32 devices in a mesh: gx: 4 (over z), gy: 8 (over y, x, core).
Axes of the slice: x: 2, y: 2, z: 4, core: 2. Of those that a mesh axis runs over, the one named last changes fastest.
Arguments:
- conductivity: bfloat16 [2, 1024, 4096], P(None, 'gy', 'gx'), may hold values from 0.099609375 to 1.59375
Outputs:
- coarse_stencil: float32 [9, 8, 64, 2048], P(None, 'gy', 'gx')
All inputs are finite; a program needn't handle non-finite values.
Results may differ from a plain program's by a relative error of at most 0.0003.
Values may be sent and summed in bfloat16 or wider, within the bound.
A program may use at most 64 MiB of HBM per device.

v0:
```python
from functools import partial

import jax
import jax.numpy as jnp
from jax import lax
from jax.sharding import PartitionSpec as P


def with_halo(cells, sides, width):
    for axis, dim in sides:
        count = lax.axis_size(axis)
        ends = count - 1
        head = lax.slice_in_dim(cells, 0, width, axis=dim)
        tail = lax.slice_in_dim(cells, cells.shape[dim] - width, cells.shape[dim], axis=dim)
        cells = jnp.concatenate(
            [
                lax.ppermute(tail, axis, [(i, (i + 1) % count) for i in range(ends)]),
                cells,
                lax.ppermute(head, axis, [((i + 1) % count, i) for i in range(ends)]),
            ],
            axis=dim,
        )
    return cells


def harmonic(first, second):
    return 2.0 * first * second / (first + second)


def prepare_window(extended, row_start, col_start, rows_all, cols_all, used_rows, used_cols):
    conduct = extended.astype(jnp.float32)
    ext_rows = conduct.shape[1]
    ext_cols = conduct.shape[2]
    row_places = jnp.arange(ext_rows, dtype=jnp.int32)
    col_places = jnp.arange(ext_cols, dtype=jnp.int32)
    row_ids = row_start - 2 + row_places
    col_ids = col_start - 2 + col_places
    row_inside = (row_ids >= 0) & (row_ids < rows_all) & (row_places < used_rows)
    col_inside = (col_ids >= 0) & (col_ids < cols_all) & (col_places < used_cols)
    inside = row_inside[:, None] & col_inside[None, :]
    safe_values = jnp.where(inside[None], conduct, 1.0)
    east_face = jnp.where(
        jnp.roll(inside, -1, 1)[None],
        harmonic(safe_values, jnp.roll(safe_values, -1, 2)),
        safe_values,
    )
    west_face = jnp.where(
        jnp.roll(inside, 1, 1)[None],
        harmonic(safe_values, jnp.roll(safe_values, 1, 2)),
        safe_values,
    )
    north_face = jnp.where(
        jnp.roll(inside, -1, 0)[None],
        harmonic(safe_values, jnp.roll(safe_values, -1, 1)),
        safe_values,
    )
    south_face = jnp.where(
        jnp.roll(inside, 1, 0)[None],
        harmonic(safe_values, jnp.roll(safe_values, 1, 1)),
        safe_values,
    )
    vertical = harmonic(safe_values[0], safe_values[1])
    centre = east_face + west_face + north_face + south_face + vertical[None] + safe_values
    col_east = east_face[0] + east_face[1]
    col_west = west_face[0] + west_face[1]
    row_north = north_face[0] + north_face[1]
    row_south = south_face[0] + south_face[1]
    left_weight = col_west / (col_west + col_east)
    right_weight = col_east / (col_west + col_east)
    south_weight = row_south / (row_south + row_north)
    north_weight = row_north / (row_south + row_north)
    odd_rows = (row_ids % 2 == 1)[:, None]
    odd_cols = (col_ids % 2 == 1)[None, :]
    even_point = inside & (row_ids % 2 == 0)[:, None] & (col_ids % 2 == 0)[None, :]
    row_class = (row_ids // 2 % 3)[:, None]
    col_class = (col_ids // 2 % 3)[None, :]
    return (
        inside,
        odd_rows,
        odd_cols,
        even_point,
        row_class,
        col_class,
        east_face,
        west_face,
        north_face,
        south_face,
        vertical,
        centre,
        left_weight,
        right_weight,
        south_weight,
        north_weight,
    )


def probe_rows(prepared, local_rows, colour):
    (
        inside,
        odd_rows,
        odd_cols,
        even_point,
        row_class,
        col_class,
        east_face,
        west_face,
        north_face,
        south_face,
        vertical,
        centre,
        left_weight,
        right_weight,
        south_weight,
        north_weight,
    ) = prepared
    chosen = even_point & (row_class == colour // 3) & (col_class == colour % 3)
    probe_field = chosen.astype(jnp.float32)
    along_x = jnp.where(
        odd_cols,
        left_weight * jnp.roll(probe_field, 1, 1) + right_weight * jnp.roll(probe_field, -1, 1),
        probe_field,
    )
    fine_field = jnp.where(
        odd_rows,
        south_weight * jnp.roll(along_x, 1, 0) + north_weight * jnp.roll(along_x, -1, 0),
        along_x,
    )
    fine_field = jnp.where(inside, fine_field, 0.0)
    applied = (
        centre * fine_field
        - east_face * jnp.roll(fine_field, -1, 1)
        - west_face * jnp.roll(fine_field, 1, 1)
        - north_face * jnp.roll(fine_field, -1, 0)
        - south_face * jnp.roll(fine_field, 1, 0)
        - vertical * fine_field
    )
    folded = jnp.where(inside, applied[0] + applied[1], 0.0)
    rows_done = (
        folded + jnp.roll(south_weight * folded, -1, 0) + jnp.roll(north_weight * folded, 1, 0)
    )
    cols_done = (
        rows_done
        + jnp.roll(left_weight * rows_done, -1, 1)
        + jnp.roll(right_weight * rows_done, 1, 1)
    )
    width = cols_done.shape[1]
    kept = cols_done[2 : 2 + local_rows].reshape(local_rows // 2, 2, width)
    return kept[:, 0]


def by_offset(colours, row_first, col_first):
    count_rows = colours.shape[1]
    count_cols = colours.shape[2]
    coarse_rows = row_first + jnp.arange(count_rows, dtype=jnp.int32)
    coarse_cols = col_first + jnp.arange(count_cols, dtype=jnp.int32)
    fields = []
    for step_row in (-1, 0, 1):
        for step_col in (-1, 0, 1):
            row_group = (coarse_rows + step_row) % 3
            col_group = (coarse_cols + step_col) % 3
            selected = jnp.zeros((count_rows, count_cols), jnp.float32)
            for colour in range(9):
                chosen = (row_group == colour // 3)[:, None] & (col_group == colour % 3)[None, :]
                selected = jnp.where(chosen, colours[colour], selected)
            fields.append(selected)
    return jnp.stack(fields)


def shards(conductivity):
    local_rows = conductivity.shape[1]
    local_cols = conductivity.shape[2]
    row_start = lax.axis_index("gy") * local_rows
    col_start = lax.axis_index("gx") * local_cols
    rows_all = local_rows * lax.axis_size("gy")
    cols_all = local_cols * lax.axis_size("gx")
    extended = with_halo(conductivity, (("gx", 2), ("gy", 1)), 2)
    used_rows = local_rows + 4
    used_cols = local_cols + 4
    row_fill = -used_rows % 8
    col_fill = -used_cols % 128
    aligned = jnp.pad(extended, ((0, 0), (0, row_fill), (0, col_fill)))
    prepared = prepare_window(
        aligned, row_start, col_start, rows_all, cols_all, used_rows, used_cols
    )
    row_picked = lax.map(partial(probe_rows, prepared, local_rows), jnp.arange(9, dtype=jnp.int32))
    width = row_picked.shape[2]
    half_cols = local_cols // 2
    picker = (
        jnp.arange(width, dtype=jnp.int32)[:, None]
        == 2 + 2 * jnp.arange(half_cols, dtype=jnp.int32)[None, :]
    ).astype(jnp.float32)
    flat_rows = row_picked.reshape(9 * (local_rows // 2), width)
    colours = jnp.dot(
        flat_rows, picker, precision=lax.Precision.HIGHEST, preferred_element_type=jnp.float32
    )
    colours = colours.reshape(9, local_rows // 2, half_cols)
    stencil = by_offset(colours, row_start // 2, col_start // 2)
    moved = lax.all_to_all(stencil, "gx", split_axis=1, concat_axis=2, tiled=True)
    return moved[:, None]


def solution(mesh):
    in_specs = (P(None, "gy", "gx"),)
    out_specs = P(None, "gy", "gx", None)
    return jax.shard_map(shards, mesh=mesh, in_specs=in_specs, out_specs=out_specs, check_vma=False)
```

profile of v0, /device:TPU:0, one launch (start us, length us, event | category | flops | bytes accessed | tf_op | source)
XLA Modules:
  0.0 210.2 jit_solution(8876209915577884419)
XLA Ops:
  0.0 1.0 fusion.78
  1.0 5.0 %collective-permute-start = (bf16[2,128,2]{2,1,0:T(8,128)(2,1)S(1)}, bf16[2,128,2]{2,1,0:T(8,128)(2,1)S(1)}, u32[]{:S(2)}, u32[]{:S(2)}) collective-permute-start(bf16[2,128,2]{2,1,0:T(8,128)(2,1)S(1)} %get-tuple-element.442), channel_id=1, source_target_pairs={{0,8},{8,16},{16,24},{1,9},{9,17},{17,25},{2,10},{10,18},{18,26},{... | collective-permute-start | bytes 3080 | tf_op jit(solution)/shard_map/ppermute | solution.py:17
  5.9 1.3 collective-permute-start.1
  8.6 3.5 %collective-permute-done.1 = bf16[2,128,2]{2,1,0:T(8,128)(2,1)S(1)} collective-permute-done((bf16[2,128,2]{2,1,0:T(8,128)(2,1)S(1)}, bf16[2,128,2]{2,1,0:T(8,128)(2,1)S(1)}, u32[]{:S(2)}, u32[]{:S(2)}) %collective-permute-start.1) | collective-permute-done | bytes 1056 | tf_op jit(solution)/shard_map/ppermute | solution.py:19
  12.7 1.3 collective-permute-start.2
  14.0 1.3 collective-permute-start.3
  15.4 3.5 %collective-permute-done.3 = bf16[2,2,1028]{2,1,0:T(2,128)(2,1)S(1)} collective-permute-done((bf16[2,2,1028]{2,1,0:T(2,128)(2,1)S(1)}, bf16[2,2,1028]{2,1,0:T(2,128)(2,1)S(1)}, u32[]{:S(2)}, u32[]{:S(2)}) %collective-permute-start.3) | collective-permute-done | bytes 8256 | tf_op jit(solution)/shard_map/ppermute | solution.py:19
  19.9 0.9 fusion.39
  20.9 4.2 %add_add_fusion = (f32[2,136,1152]{2,1,0:T(8,128)}, f32[2,136,1152]{2,1,0:T(8,128)S(1)}, f32[2,136,1152]{2,1,0:T(8,128)S(1)}, f32[2,136,1152]{2,1,0:T(8,128)S(1)}, f32[2,136,1152]{2,1,0:T(8,128)S(1)}) fusion(f32[136,1152]{1,0:T(8,128)S(1)} %divide_bitcast_fusion, pred[136,1152]{1,0:T(8,128)(4,1)S(1)} %broadcast_and_fusion, ...), kind=kLoop, calls=%fused_computation.66 | loop fusion | flops 13160448 | bytes 13233216 | tf_op jit(solution)/shard_map/add | solution.py:63
  25.2 0.9 copy-done
  27.4 121.1 %while.14 = (s32[]{:T(128)}, f32[9,64,1152]{2,1,0:T(8,128)}, s32[9]{0:T(128)S(1)}, f32[136,1152]{1,0:T(8,128)S(1)}, f32[136,1152]{1,0:T(8,128)S(1)}, /*index=5*/...) while((s32[]{:T(128)}, f32[9,64,1152]{2,1,0:T(8,128)}, ...), condition=%wide.region_1.2_spmd.clone.clone, body=%wide.region_0.1_spmd.clone.clone.sunk | while | flops 10339566 | bytes 78140304 | solution.py:185
  30.9 1.4 fusion.104
  33.3 0.8 copy-done.8
  37.6 1.2 reshape.701
  38.8 1.3 slice_bitcast_fusion.2
  44.4 1.4 fusion.104
  46.7 0.8 copy-done.8
  51.1 1.2 reshape.701
  52.2 1.3 slice_bitcast_fusion.2
  57.8 1.4 fusion.104
  64.5 1.2 reshape.701
  65.7 1.3 slice_bitcast_fusion.2
  71.3 1.4 fusion.104
  73.6 0.8 copy-done.8
  78.0 1.2 reshape.701
  79.1 1.3 slice_bitcast_fusion.2
  84.7 1.4 fusion.104
  87.1 0.8 copy-done.8
  91.4 1.2 reshape.701
  92.6 1.3 slice_bitcast_fusion.2
  98.2 1.4 fusion.104
  100.5 0.8 copy-done.8
  104.9 1.2 reshape.701
  106.0 1.3 slice_bitcast_fusion.2
  111.6 1.4 fusion.104
  114.0 0.8 copy-done.8
  118.4 1.2 reshape.701
  119.5 1.3 slice_bitcast_fusion.2
  125.1 1.4 fusion.104
  127.4 0.8 copy-done.8
  131.8 1.2 reshape.701
  133.0 1.3 slice_bitcast_fusion.2
  138.5 1.4 fusion.104
  145.3 1.2 reshape.701
  146.4 1.3 slice_bitcast_fusion.2
  148.5 4.3 %fusion.23 = f32[576,512]{1,0:T(8,128)S(1)} fusion(f32[576,1152]{1,0:T(8,128)} %bitcast.88, s32[512]{0:T(512)S(1)} %multiply_add_fusion), kind=kOutput, calls=%fused_computation.55 | convolution fusion | flops 4077453312 | bytes 3835904 | tf_op jit(solution)/shard_map/dot_general | solution.py:193
  155.4 52.3 %all_to_all.15 = f32[9,64,512]{2,0,1:T(8,128)S(1)} all-to-all(f32[9,64,512]{2,0,1:T(8,128)S(1)} %copy.7), channel_id=1, replica_groups=mesh['gx'=4,'gy'=8] {'gx'}, dimensions={1} | all-to-all | bytes 2359296 | tf_op jit(solution)/shard_map/all_to_all | solution.py:198
  208.4 1.8 broadcast_in_dim.97
  (409 shorter events, 71.5 us)
Async XLA Ops:
  1.0 7.6 %collective-permute-start = (bf16[2,128,2]{2,1,0:T(8,128)(2,1)S(1)}, bf16[2,128,2]{2,1,0:T(8,128)(2,1)S(1)}, u32[]{:S(2)}, u32[]{:S(2)}) collective-permute-start(bf16[2,128,2]{2,1,0:T(8,128)(2,1)S(1)} %get-tuple-element.442), channel_id=1, source_target_pairs={{0,8},{8,16},{16,24},{1,9},{9,17},{17,25},{2,10},{10,18},{18,26},{... | collective-permute-start | bytes 3080 | tf_op jit(solution)/shard_map/ppermute | solution.py:17
  5.9 6.2 %collective-permute-start.1 = (bf16[2,128,2]{2,1,0:T(8,128)(2,1)S(1)}, bf16[2,128,2]{2,1,0:T(8,128)(2,1)S(1)}, u32[]{:S(2)}, u32[]{:S(2)}) collective-permute-start(bf16[2,128,2]{2,1,0:T(8,128)(2,1)S(1)} %get-tuple-element.441), channel_id=1, source_target_pairs={{8,0},{16,8},{24,16},{9,1},{17,9},{25,17},{10,2},{18,10},{26,18},{... | collective-permute-start | bytes 3080 | tf_op jit(solution)/shard_map/ppermute | solution.py:19
  7.4 4.7 %copy-start.9 = (bf16[2,128,1024]{2,1,0:T(8,128)(2,1)S(1)}, bf16[2,128,1024]{2,1,0:T(8,128)(2,1)}, u32[]{:S(2)}) copy-start(bf16[2,128,1024]{2,1,0:T(8,128)(2,1)} %param.3) | copy-start | bytes 1572868
  12.7 2.6 %collective-permute-start.2 = (bf16[2,2,1028]{2,1,0:T(2,128)(2,1)S(1)}, bf16[2,2,1028]{2,1,0:T(2,128)(2,1)S(1)}, u32[]{:S(2)}, u32[]{:S(2)}) collective-permute-start(bf16[2,2,1028]{2,1,0:T(2,128)(2,1)S(1)} %get-tuple-element.439), channel_id=1, source_target_pairs={{0,1},{1,2},{2,3},{3,4},{4,5},{5,6},{6,7},{8,9},{9,10},{10,11},{11... | collective-permute-start | bytes 24680 | tf_op jit(solution)/shard_map/ppermute | solution.py:17
  14.0 4.8 %collective-permute-start.3 = (bf16[2,2,1028]{2,1,0:T(2,128)(2,1)S(1)}, bf16[2,2,1028]{2,1,0:T(2,128)(2,1)S(1)}, u32[]{:S(2)}, u32[]{:S(2)}) collective-permute-start(bf16[2,2,1028]{2,1,0:T(2,128)(2,1)S(1)} %get-tuple-element.440), channel_id=1, source_target_pairs={{1,0},{2,1},{3,2},{4,3},{5,4},{6,5},{7,6},{9,8},{10,9},{11,10},{12... | collective-permute-start | bytes 24680 | tf_op jit(solution)/shard_map/ppermute | solution.py:19
  25.0 1.5 copy-start.2
  25.0 2.0 copy-start.4
  25.0 2.3 %copy-start.6 = (f32[2,136,1152]{2,1,0:T(8,128)}, f32[2,136,1152]{2,1,0:T(8,128)S(1)}, u32[]{:S(2)}) copy-start(f32[2,136,1152]{2,1,0:T(8,128)S(1)} %get-tuple-element.647) | copy-start | bytes 3760132
  32.8 1.3 copy-start.8
  33.0 1.5 copy-start.5
  33.0 1.9 copy-start.7
  33.1 2.2 %copy-start.1 = (f32[2,136,1152]{2,1,0:T(8,128)S(1)}, f32[2,136,1152]{2,1,0:T(8,128)}, u32[]{:S(2)}) copy-start(f32[2,136,1152]{2,1,0:T(8,128)} %get-tuple-element.698) | copy-start | bytes 3760132 | tf_op jit(solution)/shard_map/while
  33.1 2.5 %copy-start.3 = (f32[2,136,1152]{2,1,0:T(8,128)S(1)}, f32[2,136,1152]{2,1,0:T(8,128)}, u32[]{:S(2)}) copy-start(f32[2,136,1152]{2,1,0:T(8,128)} %get-tuple-element.699) | copy-start | bytes 3760132 | tf_op jit(solution)/shard_map/while
  46.5 1.5 copy-start.5
  46.5 1.9 copy-start.7
  46.6 2.2 %copy-start.1 = (f32[2,136,1152]{2,1,0:T(8,128)S(1)}, f32[2,136,1152]{2,1,0:T(8,128)}, u32[]{:S(2)}) copy-start(f32[2,136,1152]{2,1,0:T(8,128)} %get-tuple-element.698) | copy-start | bytes 3760132 | tf_op jit(solution)/shard_map/while
  46.6 2.5 %copy-start.3 = (f32[2,136,1152]{2,1,0:T(8,128)S(1)}, f32[2,136,1152]{2,1,0:T(8,128)}, u32[]{:S(2)}) copy-start(f32[2,136,1152]{2,1,0:T(8,128)} %get-tuple-element.699) | copy-start | bytes 3760132 | tf_op jit(solution)/shard_map/while
  59.9 1.5 copy-start.5
  59.9 1.9 copy-start.7
  60.0 2.2 %copy-start.1 = (f32[2,136,1152]{2,1,0:T(8,128)S(1)}, f32[2,136,1152]{2,1,0:T(8,128)}, u32[]{:S(2)}) copy-start(f32[2,136,1152]{2,1,0:T(8,128)} %get-tuple-element.698) | copy-start | bytes 3760132 | tf_op jit(solution)/shard_map/while
  60.0 2.5 %copy-start.3 = (f32[2,136,1152]{2,1,0:T(8,128)S(1)}, f32[2,136,1152]{2,1,0:T(8,128)}, u32[]{:S(2)}) copy-start(f32[2,136,1152]{2,1,0:T(8,128)} %get-tuple-element.699) | copy-start | bytes 3760132 | tf_op jit(solution)/shard_map/while
  73.1 1.3 copy-start.8
  73.4 1.5 copy-start.5
  73.4 1.9 copy-start.7
  73.5 2.2 %copy-start.1 = (f32[2,136,1152]{2,1,0:T(8,128)S(1)}, f32[2,136,1152]{2,1,0:T(8,128)}, u32[]{:S(2)}) copy-start(f32[2,136,1152]{2,1,0:T(8,128)} %get-tuple-element.698) | copy-start | bytes 3760132 | tf_op jit(solution)/shard_map/while
  73.5 2.5 %copy-start.3 = (f32[2,136,1152]{2,1,0:T(8,128)S(1)}, f32[2,136,1152]{2,1,0:T(8,128)}, u32[]{:S(2)}) copy-start(f32[2,136,1152]{2,1,0:T(8,128)} %get-tuple-element.699) | copy-start | bytes 3760132 | tf_op jit(solution)/shard_map/while
  86.6 1.3 copy-start.8
  86.8 1.5 copy-start.5
  86.8 1.9 copy-start.7
  86.9 2.2 %copy-start.1 = (f32[2,136,1152]{2,1,0:T(8,128)S(1)}, f32[2,136,1152]{2,1,0:T(8,128)}, u32[]{:S(2)}) copy-start(f32[2,136,1152]{2,1,0:T(8,128)} %get-tuple-element.698) | copy-start | bytes 3760132 | tf_op jit(solution)/shard_map/while
  86.9 2.5 %copy-start.3 = (f32[2,136,1152]{2,1,0:T(8,128)S(1)}, f32[2,136,1152]{2,1,0:T(8,128)}, u32[]{:S(2)}) copy-start(f32[2,136,1152]{2,1,0:T(8,128)} %get-tuple-element.699) | copy-start | bytes 3760132 | tf_op jit(solution)/shard_map/while
  100.0 1.3 copy-start.8
  100.3 1.5 copy-start.5
  100.3 1.9 copy-start.7
  100.4 2.2 %copy-start.1 = (f32[2,136,1152]{2,1,0:T(8,128)S(1)}, f32[2,136,1152]{2,1,0:T(8,128)}, u32[]{:S(2)}) copy-start(f32[2,136,1152]{2,1,0:T(8,128)} %get-tuple-element.698) | copy-start | bytes 3760132 | tf_op jit(solution)/shard_map/while
  100.4 2.5 %copy-start.3 = (f32[2,136,1152]{2,1,0:T(8,128)S(1)}, f32[2,136,1152]{2,1,0:T(8,128)}, u32[]{:S(2)}) copy-start(f32[2,136,1152]{2,1,0:T(8,128)} %get-tuple-element.699) | copy-start | bytes 3760132 | tf_op jit(solution)/shard_map/while
  113.7 1.5 copy-start.5
  113.7 1.9 copy-start.7
  113.9 2.2 %copy-start.1 = (f32[2,136,1152]{2,1,0:T(8,128)S(1)}, f32[2,136,1152]{2,1,0:T(8,128)}, u32[]{:S(2)}) copy-start(f32[2,136,1152]{2,1,0:T(8,128)} %get-tuple-element.698) | copy-start | bytes 3760132 | tf_op jit(solution)/shard_map/while
  113.9 2.5 %copy-start.3 = (f32[2,136,1152]{2,1,0:T(8,128)S(1)}, f32[2,136,1152]{2,1,0:T(8,128)}, u32[]{:S(2)}) copy-start(f32[2,136,1152]{2,1,0:T(8,128)} %get-tuple-element.699) | copy-start | bytes 3760132 | tf_op jit(solution)/shard_map/while
  127.2 1.5 copy-start.5
  127.2 1.9 copy-start.7
  127.3 2.2 %copy-start.1 = (f32[2,136,1152]{2,1,0:T(8,128)S(1)}, f32[2,136,1152]{2,1,0:T(8,128)}, u32[]{:S(2)}) copy-start(f32[2,136,1152]{2,1,0:T(8,128)} %get-tuple-element.698) | copy-start | bytes 3760132 | tf_op jit(solution)/shard_map/while
  127.3 2.5 %copy-start.3 = (f32[2,136,1152]{2,1,0:T(8,128)S(1)}, f32[2,136,1152]{2,1,0:T(8,128)}, u32[]{:S(2)}) copy-start(f32[2,136,1152]{2,1,0:T(8,128)} %get-tuple-element.699) | copy-start | bytes 3760132 | tf_op jit(solution)/shard_map/while
  140.6 1.5 copy-start.5
  140.6 1.9 copy-start.7
  140.8 2.2 %copy-start.1 = (f32[2,136,1152]{2,1,0:T(8,128)S(1)}, f32[2,136,1152]{2,1,0:T(8,128)}, u32[]{:S(2)}) copy-start(f32[2,136,1152]{2,1,0:T(8,128)} %get-tuple-element.698) | copy-start | bytes 3760132 | tf_op jit(solution)/shard_map/while
  140.8 2.5 %copy-start.3 = (f32[2,136,1152]{2,1,0:T(8,128)S(1)}, f32[2,136,1152]{2,1,0:T(8,128)}, u32[]{:S(2)}) copy-start(f32[2,136,1152]{2,1,0:T(8,128)} %get-tuple-element.699) | copy-start | bytes 3760132 | tf_op jit(solution)/shard_map/while
  (6 other events, 7.5 us)
where the time goes:
time: 212 us; the launch traced here: 210 us
  local copies, waits for them, and re-layouts  74.1 us (35%)
  blocking collectives  52.3 us (25%)
  other arithmetic  46.5 us (22%)
  loops' own time  16.9 us (8%)
  starting transfers between devices  8.83 us (4%)
  waiting for transfers between devices  6.95 us (3%)
  matrix products  4.32 us (2%)
    all_to_all x1, blocking collectives, shards(): lax.all_to_all(stencil, 'gx', split_axis=1, concat_axis=2, tiled=True)  52.3 us
    while x90, local copies, waits for them, and re-layouts  21.7 us
    another operation x1, loops' own time, shards(): lax.map(partial(probe_rows, prepared, local_rows), jnp.arange(9, dtype=jn...  16.9 us
    mul x9, other arithmetic, probe_rows(): vertical * fine_field  12.9 us
    broadcast_in_dim x9, local copies, waits for them, and re-layouts, shards(): lax.map(partial(probe_rows, prepared, local_rows), jnp.arange(9, dtype=jn...  11.4 us
    reshape x9, local copies, waits for them, and re-layouts, probe_rows(): kept = cols_done[2:2 + local_rows].reshape(local_rows // 2, 2, width)  10.5 us
    sub x9, other arithmetic, probe_rows(): centre * fine_field - east_face * jnp.roll(fine_field, -1, 1)  6.98 us
    ppermute x2, waiting for transfers between devices, with_halo(): lax.ppermute(head, axis, [((i + 1) % count, i) for i in range(ends)])  6.95 us
  transfers between devices with their start and end apart: 4, of which 2 were waited for; matrix products, arithmetic and copies ran while one was open for 1% of the time, Pallas kernels for 0%

commit v1 on v0

v1 whole, which is shorter than its diff:
```python
import functools

import jax
import jax.numpy as jnp
from jax import lax
from jax.experimental import pallas as pl
from jax.experimental.pallas import tpu as pltpu
from jax.sharding import PartitionSpec as P

MESH = pl.DeviceIdType.MESH
LANES = 128


def gather_kernel(
    n, m, cells, main, mid, edge, tails, heads, pack, main_send, main_recv, mid_send, mid_recv, edge_send, edge_recv, own
):
    i = lax.axis_index("gx")
    j = lax.axis_index("gy")
    band = main.shape[2]
    takes_south = (i == 0) & (j > 0)
    takes_north = (i == n - 1) & (j < m - 1)
    before = jnp.maximum(j - 1, 0)
    after = jnp.minimum(j + 1, m - 1)

    barrier = pltpu.get_barrier_semaphore()

    def greet(x, y):
        pl.semaphore_signal(barrier, inc=1, device_id=(x, y), device_id_type=MESH)

    for d in range(1, n):
        greet(lax.rem(i + d, n), j)

    @pl.when(takes_south)
    def _():
        for k in range(n):
            greet(k, before)

    @pl.when(takes_north)
    def _():
        for k in range(n):
            greet(k, after)

    loads = []
    for t in range(n):
        loads.append(pltpu.make_async_copy(cells.at[:, pl.ds(t * band + band - 8, 8), :], tails.at[t], own.at[2 * t]))
        loads.append(pltpu.make_async_copy(cells.at[:, pl.ds(t * band, 8), :], heads.at[t], own.at[2 * t + 1]))
    for load in loads:
        load.start()
    for load in loads:
        load.wait()
    sub = lax.broadcasted_iota(jnp.int32, (8, cells.shape[2]), 0)
    for u in range(n + 2):
        under, over = min(max(u - 2, 0), n - 1), min(u, n - 1)
        low = [pltpu.roll(tails[under, p].astype(jnp.float32), 2 + 2 * p, 0) for p in range(2)]
        high = [pltpu.roll(heads[over, p].astype(jnp.float32), 4 + p, 0) for p in range(2)]
        rows = jnp.where(sub < 2, low[0], jnp.where(sub < 4, low[1], jnp.where(sub == 4, high[0], high[1])))
        pack[u] = rows.astype(jnp.bfloat16)

    @pl.when(jnp.logical_not(takes_south | takes_north))
    def _():
        edge[...] = jnp.ones(edge.shape, edge.dtype)

    north, south = jnp.where(j < m - 1, 1, 0), jnp.where(j > 0, 1, 0)
    pl.semaphore_wait(barrier, n - 1 + north + south)

    def remote(src, dst, send, recv, x, y):
        return pltpu.make_async_remote_copy(
            src_ref=src, dst_ref=dst, send_sem=send, recv_sem=recv, device_id=(x, y), device_id_type=MESH
        )

    def rows_of(t):
        return cells.at[:, pl.ds(pl.multiple_of(t * band, band), band), :]

    def main_copy(d):
        t = lax.rem(i + d, n)
        return remote(rows_of(t), main.at[i], main_send.at[d], main_recv.at[i], t, j)

    def mid_copy(d):
        t = lax.rem(i + d, n)
        return remote(pack.at[t + 1], mid.at[i], mid_send.at[d], mid_recv.at[i], t, j)

    def edge_north():
        return remote(pack.at[n + 1], edge.at[i], edge_send.at[0], edge_recv.at[i], 0, after)

    def edge_south():
        return remote(pack.at[0], edge.at[i], edge_send.at[1], edge_recv.at[i], n - 1, before)

    order = [n // 2] + [d for d in range(1, n) if d != n // 2]
    for d in order:
        main_copy(d).start()
    for d in order:
        mid_copy(d).start()

    @pl.when(j < m - 1)
    def _():
        edge_north().start()

    @pl.when(j > 0)
    def _():
        edge_south().start()

    own_main = pltpu.make_async_copy(rows_of(i), main.at[i], own.at[0])
    own_main.start()
    own_mid = pltpu.make_async_copy(pack.at[i + 1], mid.at[i], own.at[1])
    own_mid.start()
    own_main.wait()
    own_mid.wait()
    for d in range(1, n):
        k = lax.rem(i + d, n)
        remote(rows_of(0), main.at[k], main_send.at[d], main_recv.at[k], k, j).wait_recv()
        remote(pack.at[0], mid.at[k], mid_send.at[d], mid_recv.at[k], k, j).wait_recv()

    @pl.when(takes_south | takes_north)
    def _():
        for k in range(n):
            remote(pack.at[0], edge.at[k], edge_send.at[0], edge_recv.at[k], i, after).wait_recv()

    for d in range(1, n):
        main_copy(d).wait_send()
        mid_copy(d).wait_send()

    @pl.when(j < m - 1)
    def _():
        edge_north().wait_send()

    @pl.when(j > 0)
    def _():
        edge_south().wait_send()


def face(x0, y0, x1, y1):
    s0, s1 = x0 + y0, x1 + y1
    return 2.0 * (x0 * y0 * s1 + x1 * y1 * s0) / (s0 * s1)


def with_vertical(sides, wall, k0, k1):
    vertical = 2.0 * (2.0 * k0 * k1 / (k0 + k1))
    return (sides + (wall + vertical)) - vertical


def stencil_kernel(n, m, main, mid, edge, out, cell, weights):
    band = main.shape[2]
    block = main.shape[3]
    half = band // 2
    rows = cell.shape[2]
    tiles = out.shape[2] // LANES
    per_block = block // (2 * LANES)
    i = lax.axis_index("gx")
    j = lax.axis_index("gy")
    first_rows = (i == 0) & (j == 0)
    last_rows = (i == n - 1) & (j == m - 1)

    taken = 2 * band + 16
    want = lax.broadcasted_iota(jnp.int32, (4 * rows, taken), 0)
    have = lax.broadcasted_iota(jnp.int32, (4 * rows, taken), 1)
    group = jnp.where(want >= 3 * rows, 3, jnp.where(want >= 2 * rows, 2, jnp.where(want >= rows, 1, 0)))
    place = want - group * rows
    plane = jnp.where(group >= 2, 1, 0)
    odd = group - 2 * plane
    inside = plane * band + 2 * jnp.where(place < half, place, 0) + odd
    above = jnp.where(odd == 0, 2 * band + jnp.where(i == n - 1, 8, 0) + 4 + plane, plane * band + 1)
    below = 2 * band + jnp.where(i == 0, 8, 0) + 2 * plane + odd
    source = jnp.where(place == half, above, jnp.where(place == rows - 1, below, inside))
    pick_rows = jnp.where(have == source, 1.0, 0.0).astype(jnp.bfloat16)
    fine = lax.broadcasted_iota(jnp.int32, (2 * LANES, 2 * LANES), 0)
    to = lax.broadcasted_iota(jnp.int32, (2 * LANES, 2 * LANES), 1)
    pick_cols = jnp.where(fine == jnp.where(to < LANES, 2 * to, 2 * (to - LANES) + 1), 1.0, 0.0).astype(jnp.bfloat16)

    lane = lax.broadcasted_iota(jnp.int32, (rows, LANES), 1)
    sub = lax.broadcasted_iota(jnp.int32, (rows, LANES), 0)
    bottom = (sub == 0) & first_rows
    top = (sub == half - 1) & last_rows

    def up(x):
        return pltpu.roll(x, rows - 1, 0)

    def down(x):
        return pltpu.roll(x, 1, 0)

    for t in range(tiles):
        k, part = divmod(t, per_block)
        cols = slice(part * 2 * LANES, (part + 1) * 2 * LANES)
        stored = jnp.concatenate(
            [
                main[k, 0, :, cols].astype(jnp.float32),
                main[k, 1, :, cols].astype(jnp.float32),
                mid[k, :, cols].astype(jnp.float32),
                edge[k, :, cols].astype(jnp.float32),
            ],
            axis=0,
        ).astype(jnp.bfloat16)
        picked = jnp.dot(pick_rows, stored, preferred_element_type=jnp.float32).astype(jnp.bfloat16)
        split = jnp.dot(picked, pick_cols, preferred_element_type=jnp.float32)
        a0, c0, a1, c1 = (split[g * rows : (g + 1) * rows, :LANES] for g in range(4))
        b0, d0, b1, d1 = (split[g * rows : (g + 1) * rows, LANES:] for g in range(4))
        for at, value in enumerate((a0, a1, b0, b1, c0, c1, d0, d1)):
            cell[t, at] = value
        v1 = face(a0, c0, a1, c1)
        v2 = jnp.where(top, c0 + c1, face(c0, up(a0), c1, up(a1)))
        total = 1.0 / (v1 + v2)
        north = v2 * total
        weights[t, 0] = v1 * total
        weights[t, 1] = north
        weights[t, 2] = v1 * north
    ones = jnp.ones((rows, LANES), jnp.float32)
    for at in range(8):
        cell[tiles, at] = ones
    for at in range(3):
        weights[tiles, at] = ones

    def step(t, carry):
        last = (lane == LANES - 1) & (t == tiles - 1)
        first = (lane == 0) & (t == 0)

        def ahead(ref, at):
            return pltpu.roll(jnp.where(lane == 0, ref[t + 1, at], ref[t, at]), LANES - 1, 1)

        rolled = []

        def behind(x):
            turned = pltpu.roll(x, 1, 1)
            before = carry[len(rolled)]
            rolled.append(turned)
            return jnp.where(lane == 0, before, turned)

        a0, a1, b0, b1, c0, c1, d0, d1 = (cell[t, at] for at in range(8))
        s0, n0, t0 = (weights[t, at] for at in range(3))
        wall_a, wall_b, wall_c, wall_d = a0 + a1, b0 + b1, c0 + c1, d0 + d1
        h1 = face(a0, b0, a1, b1)
        h2 = jnp.where(last, wall_b, face(b0, ahead(cell, 0), b1, ahead(cell, 1)))
        g1 = face(c0, d0, c1, d1)
        g2 = jnp.where(last, wall_d, face(d0, ahead(cell, 4), d1, ahead(cell, 5)))
        w1 = face(b0, d0, b1, d1)
        w2 = jnp.where(top, wall_d, face(d0, up(b0), d1, up(b1)))
        total = 1.0 / (w1 + w2)
        s1 = w1 * total
        n1 = w2 * total
        t1 = w1 * n1
        total = 1.0 / (h1 + h2)
        left = h1 * total
        right = h2 * total
        left_up = up(left)
        right_up = up(right)
        s0_next = ahead(weights, 0)
        n0_next = ahead(weights, 1)

        side_a = with_vertical(h1 + jnp.where(first, wall_a, behind(h2)), wall_a, a0, a1)
        side_c = with_vertical(g1 + jnp.where(first, wall_c, behind(g2)), wall_c, c0, c1)
        side_b = with_vertical(h1 + h2, wall_b, b0, b1)
        side_d = with_vertical(g1 + g2, wall_d, d0, d1)

        nc = n0 * side_c
        sc = s0 * side_c
        nd = n1 * side_d
        sd = s1 * side_d
        even = side_a + t0 + s0 * sc + jnp.where(bottom, wall_a, down(t0 + n0 * nc))
        odd_ = side_b + t1 + s1 * sd + jnp.where(bottom, wall_b, down(t1 + n1 * nd))
        even_up = s0 * nc - t0
        odd_up = s1 * nd - t1
        sg = s0 * g1
        ng = n0 * g1
        sq = s0_next * g2
        nq = n0_next * g2
        p = h1 + s1 * sg + jnp.where(bottom, 0.0, down(n1 * ng))
        q = h2 + s1 * sq + jnp.where(bottom, 0.0, down(n1 * nq))
        p_up = n1 * sg
        p_down = s1 * ng
        q_up = s1 * nq
        q_down = n1 * sq

        mid = left * odd_ - p
        east = jnp.where(last, 0.0, right * mid - left * q)
        centre = even + left * (mid - p) + behind(right * (right * odd_ - 2.0 * q))
        lo = left * odd_up - p_up
        ro = right * odd_up - q_down
        north = even_up + left_up * lo - left * p_down + behind(right_up * ro - right * q_up)
        north = jnp.where(top, 0.0, north)
        north_east = jnp.where(last | top, 0.0, right_up * lo - left * q_up)
        north_west = jnp.where(last | top, 0.0, left_up * ro - right * p_down)
        west = behind(east)
        ne_back = behind(north_east)
        nw_back = behind(north_west)
        cols = pl.ds(pl.multiple_of(t * LANES, LANES), LANES)

        def below(x):
            return jnp.where(bottom, 0.0, down(x))

        for at, value in enumerate(
            (below(ne_back), below(north), below(north_west), west, centre, east, nw_back, north, north_east)
        ):
            out[at, :, cols] = value[:half]
        return tuple(rolled)

    zero = jnp.zeros((rows, LANES), jnp.float32)
    lax.fori_loop(0, tiles, step, (zero,) * 7)


def shards(n, m, conductivity):
    planes, local_rows, local_cols = conductivity.shape
    band = local_rows // n
    half = band // 2
    rows = -(-(half + 2) // 8) * 8
    tiles = n * local_cols // (2 * LANES)
    vmem = pl.BlockSpec(memory_space=pltpu.VMEM)
    anywhere = pl.BlockSpec(memory_space=pl.ANY)
    dma = pltpu.SemaphoreType.DMA
    main, mid, edge = pl.pallas_call(
        functools.partial(gather_kernel, n, m),
        out_shape=(
            jax.ShapeDtypeStruct((n, planes, band, local_cols), jnp.bfloat16),
            jax.ShapeDtypeStruct((n, 8, local_cols), jnp.bfloat16),
            jax.ShapeDtypeStruct((n, 8, local_cols), jnp.bfloat16),
        ),
        in_specs=[anywhere],
        out_specs=(vmem, vmem, vmem),
        scratch_shapes=[
            pltpu.VMEM((n, planes, 8, local_cols), jnp.bfloat16),
            pltpu.VMEM((n, planes, 8, local_cols), jnp.bfloat16),
            pltpu.VMEM((n + 2, 8, local_cols), jnp.bfloat16),
            dma((n,)),
            dma((n,)),
            dma((n,)),
            dma((n,)),
            dma((2,)),
            dma((n,)),
            dma((2 * n,)),
        ],
        compiler_params=pltpu.CompilerParams(collective_id=0, has_side_effects=True),
        name="gather_rows",
    )(conductivity)
    stencil = pl.pallas_call(
        functools.partial(stencil_kernel, n, m),
        out_shape=jax.ShapeDtypeStruct((9, half, tiles * LANES), jnp.float32),
        in_specs=[vmem, vmem, vmem],
        out_specs=vmem,
        scratch_shapes=[
            pltpu.VMEM((tiles + 1, 8, rows, LANES), jnp.float32),
            pltpu.VMEM((tiles + 1, 3, rows, LANES), jnp.float32),
        ],
        name="stencil",
    )(main, mid, edge)
    return stencil[:, None]


def solution(mesh):
    n, m = mesh.shape["gx"], mesh.shape["gy"]
    return jax.shard_map(
        functools.partial(shards, n, m),
        mesh=mesh,
        in_specs=(P(None, "gy", "gx"),),
        out_specs=P(None, "gy", "gx", None),
        check_vma=False,
    )
```

time: 212 us -> 27.7 us (0.13)
  local copies, waits for them, and re-layouts: 74.1 us -> 0 us
  blocking collectives: 52.3 us -> 0 us
  other arithmetic: 46.5 us -> 0 us
  Pallas kernels: 0 us -> 27.4 us
  loops' own time: 16.9 us -> 0 us
  starting transfers between devices: 8.83 us -> 0 us
  waiting for transfers between devices: 6.95 us -> 0 us
  matrix products: 4.32 us -> 0 us
    all_to_all x1 -> x0, blocking collectives: 52.3 us -> none  [shards(): lax.all_to_all(stencil, 'gx', split_axis=1, concat_axis=2, tiled=True)]
    pallas_call x0 -> x2, Pallas kernels: none -> 27.4 us  [the longest x1 21 us: shards(): pl.pallas_call(functools.partial(gather_kernel, n, m), out_shape=(jax.Sha...]
    while x90 -> x0, local copies, waits for them, and re-layouts: 21.7 us -> none
    mul x45 -> x0, other arithmetic: 17.4 us -> none  [the longest x9 12.9 us: probe_rows(): vertical * fine_field]
    another operation x1 -> x0, loops' own time: 16.9 us -> none  [shards(): lax.map(partial(probe_rows, prepared, local_rows), jnp.arange(9, dtype=jn...]
    broadcast_in_dim x10 -> x0, local copies, waits for them, and re-layouts: 13.2 us -> none  [the longest x9 11.4 us: shards(): lax.map(partial(probe_rows, prepared, local_rows), jnp.arange(9, dtype=jn...]
    slice x136 -> x0, local copies, waits for them, and re-layouts: 12.8 us -> none  [the longest x18 2.78 us: probe_rows(): jnp.roll(probe_field, -1, 1)]
    reshape x9 -> x0, local copies, waits for them, and re-layouts: 10.5 us -> none  [probe_rows(): kept = cols_done[2:2 + local_rows].reshape(local_rows // 2, 2, width)]
  transfers between devices with their start and end apart: 4 -> 0, of which waited for: 2 -> 0; matrix products, arithmetic and copies ran while one was open for 1% -> 0% of each run, Pallas kernels for 0% -> 0%
where the time goes in v1:
time: 27.7 us; the launch traced here: 27.4 us
  Pallas kernels  27.4 us (99%)
    pallas_call x1, Pallas kernels, shards(): pl.pallas_call(functools.partial(gather_kernel, n, m), out_shape=(jax.Sha...  21 us
    pallas_call x1, Pallas kernels, shards(): pl.pallas_call(functools.partial(stencil_kernel, n, m), out_shape=jax.Sha...  6.45 us

profile of v1, /device:TPU:0, one launch (start us, length us, event | category | flops | bytes accessed | tf_op | source)
XLA Modules:
  0.0 27.4 jit_solution(16706893468792721558)
XLA Ops:
  0.0 21.0 %gather_rows.1 = (bf16[4,2,32,1024]{3,2,1,0:T(8,128)(2,1)}, bf16[4,8,1024]{2,1,0:T(8,128)(2,1)}, bf16[4,8,1024]{2,1,0:T(8,128)(2,1)}) custom-call(bf16[2,128,1024]{2,1,0:T(8,128)(2,1)} %cells.1), custom_call_target="tpu_custom_call" | custom-call | tf_op jit(solution)/shard_map/gather_rows/pallas_call | solution.py:307
  21.0 6.5 %stencil.1 = f32[9,16,2048]{2,1,0:T(8,128)} custom-call(bf16[4,2,32,1024]{3,2,1,0:T(8,128)(2,1)} %get-tuple-element.8.main, bf16[4,8,1024]{2,1,0:T(8,128)(2,1)} %get-tuple-element.9.mid, bf16[4,8,1024]{2,1,0:T(8,128)(2,1)} %get-tuple-element.10.edge), custom_call_target="tpu_custom_call" | custom-call | tf_op jit(solution)/shard_map/stencil/pallas_call | solution.py:331

commit v2 on v1

--- a/solution.py
+++ b/solution.py
@@ -11,8 +11,9 @@
 LANES = 128
 
 
-def gather_kernel(
-    n, m, cells, main, mid, edge, tails, heads, pack, main_send, main_recv, mid_send, mid_recv, edge_send, edge_recv, own
+def coarse_kernel(
+    n, m, cells, out, main, mid, edge, tails, heads, pack, fields,
+    main_send, main_recv, mid_send, mid_recv, edge_send, edge_recv, own,
 ):
     i = lax.axis_index("gx")
     j = lax.axis_index("gy")
@@ -39,6 +40,12 @@
     def _():
         for k in range(n):
             greet(k, after)
+
+    def rows_of(t):
+        return cells.at[:, pl.ds(pl.multiple_of(t * band, band), band), :]
+
+    own_main = pltpu.make_async_copy(rows_of(i), main.at[i], own.at[2 * n])
+    own_main.start()
 
     loads = []
     for t in range(n):
@@ -68,15 +75,17 @@
             src_ref=src, dst_ref=dst, send_sem=send, recv_sem=recv, device_id=(x, y), device_id_type=MESH
         )
 
-    def rows_of(t):
-        return cells.at[:, pl.ds(pl.multiple_of(t * band, band), band), :]
+    turn = jnp.where(i < n // 2, 1, n - 1)
+
+    def peer(d):
+        return lax.rem(i + turn * d, n)
 
     def main_copy(d):
-        t = lax.rem(i + d, n)
+        t = peer(d)
         return remote(rows_of(t), main.at[i], main_send.at[d], main_recv.at[i], t, j)
 
     def mid_copy(d):
-        t = lax.rem(i + d, n)
+        t = peer(d)
         return remote(pack.at[t + 1], mid.at[i], mid_send.at[d], mid_recv.at[i], t, j)
 
     def edge_north():
@@ -87,35 +96,40 @@
 
     order = [n // 2] + [d for d in range(1, n) if d != n // 2]
     for d in order:
+        mid_copy(d).start()
+
+    @pl.when(j < m - 1)
+    def _():
+        edge_north().start()
+
+    @pl.when(j > 0)
+    def _():
+        edge_south().start()
+
+    for d in order:
         main_copy(d).start()
-    for d in order:
-        mid_copy(d).start()
-
-    @pl.when(j < m - 1)
-    def _():
-        edge_north().start()
-
-    @pl.when(j > 0)
-    def _():
-        edge_south().start()
-
-    own_main = pltpu.make_async_copy(rows_of(i), main.at[i], own.at[0])
-    own_main.start()
     own_mid = pltpu.make_async_copy(pack.at[i + 1], mid.at[i], own.at[1])
     own_mid.start()
+
+    def edge_arrived(k):
+        @pl.when(takes_south | takes_north)
+        def _():
+            remote(pack.at[0], edge.at[k], edge_send.at[0], edge_recv.at[k], i, after).wait_recv()
+
+    first, second = stages(n, m, main, mid, edge, out, fields)
     own_main.wait()
     own_mid.wait()
-    for d in range(1, n):
-        k = lax.rem(i + d, n)
+    edge_arrived(i)
+    first(i)
+    for d in order:
+        k = peer(d)
+        remote(pack.at[0], mid.at[k], mid_send.at[d], mid_recv.at[k], k, j).wait_recv()
+        edge_arrived(k)
         remote(rows_of(0), main.at[k], main_send.at[d], main_recv.at[k], k, j).wait_recv()
-        remote(pack.at[0], mid.at[k], mid_send.at[d], mid_recv.at[k], k, j).wait_recv()
-
-    @pl.when(takes_south | takes_north)
-    def _():
-        for k in range(n):
-            remote(pack.at[0], edge.at[k], edge_send.at[0], edge_recv.at[k], i, after).wait_recv()
-
-    for d in range(1, n):
+        first(k)
+    second()
+
+    for d in order:
         main_copy(d).wait_send()
         mid_copy(d).wait_send()
 
@@ -133,16 +147,22 @@
     return 2.0 * (x0 * y0 * s1 + x1 * y1 * s0) / (s0 * s1)
 
 
-def with_vertical(sides, wall, k0, k1):
+def middle(one, two):
+    total = 1.0 / (one + two)
+    second = two * total
+    return one * total, second, one * second
+
+
+def with_vertical(sides, k0, k1):
     vertical = 2.0 * (2.0 * k0 * k1 / (k0 + k1))
-    return (sides + (wall + vertical)) - vertical
-
-
-def stencil_kernel(n, m, main, mid, edge, out, cell, weights):
+    return (sides + ((k0 + k1) + vertical)) - vertical
+
+
+def stages(n, m, main, mid, edge, out, fields):
     band = main.shape[2]
     block = main.shape[3]
     half = band // 2
-    rows = cell.shape[2]
+    rows = fields.shape[2]
     tiles = out.shape[2] // LANES
     per_block = block // (2 * LANES)
     i = lax.axis_index("gx")
@@ -177,9 +197,9 @@
     def down(x):
         return pltpu.roll(x, 1, 0)
 
-    for t in range(tiles):
-        k, part = divmod(t, per_block)
-        cols = slice(part * 2 * LANES, (part + 1) * 2 * LANES)
+    def tile_terms(k, part):
+        t = k * per_block + part
+        cols = pl.ds(pl.multiple_of(part * 2 * LANES, 2 * LANES), 2 * LANES)
         stored = jnp.concatenate(
             [
                 main[k, 0, :, cols].astype(jnp.float32),
@@ -193,27 +213,32 @@
         split = jnp.dot(picked, pick_cols, preferred_element_type=jnp.float32)
         a0, c0, a1, c1 = (split[g * rows : (g + 1) * rows, :LANES] for g in range(4))
         b0, d0, b1, d1 = (split[g * rows : (g + 1) * rows, LANES:] for g in range(4))
-        for at, value in enumerate((a0, a1, b0, b1, c0, c1, d0, d1)):
-            cell[t, at] = value
-        v1 = face(a0, c0, a1, c1)
-        v2 = jnp.where(top, c0 + c1, face(c0, up(a0), c1, up(a1)))
-        total = 1.0 / (v1 + v2)
-        north = v2 * total
-        weights[t, 0] = v1 * total
-        weights[t, 1] = north
-        weights[t, 2] = v1 * north
+        s0, n0, t0 = middle(face(a0, c0, a1, c1), jnp.where(top, c0 + c1, face(c0, up(a0), c1, up(a1))))
+        s1, n1, t1 = middle(face(b0, d0, b1, d1), jnp.where(top, d0 + d1, face(d0, up(b0), d1, up(b1))))
+        h1 = face(a0, b0, a1, b1)
+        g1 = face(c0, d0, c1, d1)
+        side_a = with_vertical(h1, a0, a1)
+        side_b = with_vertical(h1, b0, b1)
+        side_c = with_vertical(g1, c0, c1)
+        side_d = with_vertical(g1, d0, d1)
+        for at, value in enumerate(
+            (a0, a1, c0, c1, s0, n0, b0, b1, d0, d1, t0, s1, n1, t1, h1, g1, side_a, side_b, side_c, side_d)
+        ):
+            fields[t, at] = value
+
+    def first(k):
+        lax.fori_loop(0, per_block, lambda part, carry: (tile_terms(k, part), carry)[1], 0)
+
     ones = jnp.ones((rows, LANES), jnp.float32)
-    for at in range(8):
-        cell[tiles, at] = ones
-    for at in range(3):
-        weights[tiles, at] = ones
+    for at in range(6):
+        fields[tiles, at] = ones
 
     def step(t, carry):
         last = (lane == LANES - 1) & (t == tiles - 1)
-        first = (lane == 0) & (t == 0)
-
-        def ahead(ref, at):
-            return pltpu.roll(jnp.where(lane == 0, ref[t + 1, at], ref[t, at]), LANES - 1, 1)
+        first_lane = (lane == 0) & (t == 0)
+
+        def ahead(at):
+            return pltpu.roll(jnp.where(lane == 0, fields[t + 1, at], fields[t, at]), LANES - 1, 1)
 
         rolled = []
 
@@ -223,31 +248,20 @@
             rolled.append(turned)
             return jnp.where(lane == 0, before, turned)
 
-        a0, a1, b0, b1, c0, c1, d0, d1 = (cell[t, at] for at in range(8))
-        s0, n0, t0 = (weights[t, at] for at in range(3))
-        wall_a, wall_b, wall_c, wall_d = a0 + a1, b0 + b1, c0 + c1, d0 + d1
-        h1 = face(a0, b0, a1, b1)
-        h2 = jnp.where(last, wall_b, face(b0, ahead(cell, 0), b1, ahead(cell, 1)))
-        g1 = face(c0, d0, c1, d1)
-        g2 = jnp.where(last, wall_d, face(d0, ahead(cell, 4), d1, ahead(cell, 5)))
-        w1 = face(b0, d0, b1, d1)
-        w2 = jnp.where(top, wall_d, face(d0, up(b0), d1, up(b1)))
-        total = 1.0 / (w1 + w2)
-        s1 = w1 * total
-        n1 = w2 * total
-        t1 = w1 * n1
-        total = 1.0 / (h1 + h2)
-        left = h1 * total
-        right = h2 * total
+        a0, a1, c0, c1, s0, n0, b0, b1, d0, d1 = (fields[t, at] for at in range(10))
+        t0, s1, n1, t1, h1, g1, side_a, side_b, side_c, side_d = (fields[t, at] for at in range(10, 20))
+        wall_a, wall_b = a0 + a1, b0 + b1
+        h2 = jnp.where(last, wall_b, face(b0, ahead(0), b1, ahead(1)))
+        g2 = jnp.where(last, d0 + d1, face(d0, ahead(2), d1, ahead(3)))
+        left, right, _ = middle(h1, h2)
         left_up = up(left)
         right_up = up(right)
-        s0_next = ahead(weights, 0)
-        n0_next = ahead(weights, 1)
-
-        side_a = with_vertical(h1 + jnp.where(first, wall_a, behind(h2)), wall_a, a0, a1)
-        side_c = with_vertical(g1 + jnp.where(first, wall_c, behind(g2)), wall_c, c0, c1)
-        side_b = with_vertical(h1 + h2, wall_b, b0, b1)
-        side_d = with_vertical(g1 + g2, wall_d, d0, d1)
+        s0_next = ahead(4)
+        n0_next = ahead(5)
+        side_a = side_a + jnp.where(first_lane, wall_a, behind(h2))
+        side_c = side_c + jnp.where(first_lane, c0 + c1, behind(g2))
+        side_b = side_b + h2
+        side_d = side_d + g2
 
         nc = n0 * side_c
         sc = s0 * side_c
@@ -291,8 +305,11 @@
             out[at, :, cols] = value[:half]
         return tuple(rolled)
 
-    zero = jnp.zeros((rows, LANES), jnp.float32)
-    lax.fori_loop(0, tiles, step, (zero,) * 7)
+    def second():
+        zero = jnp.zeros((rows, LANES), jnp.float32)
+        lax.fori_loop(0, tiles, step, (zero,) * 7)
+
+    return first, second
 
 
 def shards(n, m, conductivity):
@@ -304,41 +321,32 @@
     vmem = pl.BlockSpec(memory_space=pltpu.VMEM)
     anywhere = pl.BlockSpec(memory_space=pl.ANY)
     dma = pltpu.SemaphoreType.DMA
-    main, mid, edge = pl.pallas_call(
-        functools.partial(gather_kernel, n, m),
-        out_shape=(
-            jax.ShapeDtypeStruct((n, planes, band, local_cols), jnp.bfloat16),
-            jax.ShapeDtypeStruct((n, 8, local_cols), jnp.bfloat16),
-            jax.ShapeDtypeStruct((n, 8, local_cols), jnp.bfloat16),
-        ),
+    stencil = pl.pallas_call(
+        functools.partial(coarse_kernel, n, m),
+        out_shape=jax.ShapeDtypeStruct((9, half, tiles * LANES), jnp.float32),
         in_specs=[anywhere],
-        out_specs=(vmem, vmem, vmem),
+        out_specs=vmem,
         scratch_shapes=[
+            pltpu.VMEM((n, planes, band, local_cols), jnp.bfloat16),
+            pltpu.VMEM((n, 8, local_cols), jnp.bfloat16),
+            pltpu.VMEM((n, 8, local_cols), jnp.bfloat16),
             pltpu.VMEM((n, planes, 8, local_cols), jnp.bfloat16),
             pltpu.VMEM((n, planes, 8, local_cols), jnp.bfloat16),
             pltpu.VMEM((n + 2, 8, local_cols), jnp.bfloat16),
+            pltpu.VMEM((tiles + 1, 20, rows, LANES), jnp.float32),
             dma((n,)),
             dma((n,)),
             dma((n,)),
             dma((n,)),
             dma((2,)),
             dma((n,)),
-            dma((2 * n,)),
+            dma((2 * n + 1,)),
         ],
-        compiler_params=pltpu.CompilerParams(collective_id=0, has_side_effects=True),
-        name="gather_rows",
+        compiler_params=pltpu.CompilerParams(
+            collective_id=0, has_side_effects=True, vmem_limit_bytes=24 * 1024 * 1024
+        ),
+        name="coarse",
     )(conductivity)
-    stencil = pl.pallas_call(
-        functools.partial(stencil_kernel, n, m),
-        out_shape=jax.ShapeDtypeStruct((9, half, tiles * LANES), jnp.float32),
-        in_specs=[vmem, vmem, vmem],
-        out_specs=vmem,
-        scratch_shapes=[
-            pltpu.VMEM((tiles + 1, 8, rows, LANES), jnp.float32),
-            pltpu.VMEM((tiles + 1, 3, rows, LANES), jnp.float32),
-        ],
-        name="stencil",
-    )(main, mid, edge)
     return stencil[:, None]
 
 

time: 27.7 us -> 27 us (0.975)
  Pallas kernels: 27.4 us -> 24.8 us
  local copies, waits for them, and re-layouts: 0 us -> 2.06 us
    pallas_call x2 -> x1, Pallas kernels: 27.4 us -> 24.8 us  [shards(): pl.pallas_call(functools.partial(coarse_kernel, n, m), out_shape=jax.Shap...]
    unnamed x0 -> x3, local copies, waits for them, and re-layouts: none -> 2.06 us
where the time goes in v2:
time: 27 us; the launch traced here: 26.8 us
  Pallas kernels  24.8 us (92%)
  local copies, waits for them, and re-layouts  2.06 us (8%)
    pallas_call x1, Pallas kernels, shards(): pl.pallas_call(functools.partial(coarse_kernel, n, m), out_shape=jax.Shap...  24.8 us
    unnamed x3, local copies, waits for them, and re-layouts  2.06 us

profile of v2, /device:TPU:0, one launch (start us, length us, event | category | flops | bytes accessed | tf_op | source)
XLA Modules:
  0.0 26.8 jit_solution(15859401978533628037)
XLA Ops:
  0.0 0.0 copy-start
  0.0 1.0 %copy-done = bf16[2,128,1024]{2,1,0:T(8,128)(2,1)S(1)} copy-done((bf16[2,128,1024]{2,1,0:T(8,128)(2,1)S(1)}, bf16[2,128,1024]{2,1,0:T(8,128)(2,1)}, u32[]{:S(2)}) %copy-start) | copy-done | bytes 524312
  1.0 24.8 %coarse.1 = f32[9,16,2048]{2,1,0:T(8,128)S(1)} custom-call(bf16[2,128,1024]{2,1,0:T(8,128)(2,1)S(1)} %copy-done), custom_call_target="tpu_custom_call" | custom-call | tf_op jit(solution)/shard_map/coarse/pallas_call | solution.py:324
  25.8 1.0 %copy.4 = f32[9,1,16,2048]{3,2,1,0:T(8,128)} copy(f32[9,1,16,2048]{3,2,1,0:T(8,128)S(1)} %bitcast.3) | data formatting | bytes 2359296
Async XLA Ops:
  0.0 1.0 %copy-start = (bf16[2,128,1024]{2,1,0:T(8,128)(2,1)S(1)}, bf16[2,128,1024]{2,1,0:T(8,128)(2,1)}, u32[]{:S(2)}) copy-start(bf16[2,128,1024]{2,1,0:T(8,128)(2,1)} %cells.1) | copy-start | bytes 1572868

commit v3 on v2

--- a/solution.py
+++ b/solution.py
@@ -9,10 +9,13 @@
 
 MESH = pl.DeviceIdType.MESH
 LANES = 128
+UNROLL = 4
+STEPS = 4
+VMEM_LIMIT = 16 * 1024 * 1024
 
 
 def coarse_kernel(
-    n, m, cells, out, main, mid, edge, tails, heads, pack, fields,
+    n, m, cells, fields, main, mid, edge, tails, heads, pack,
     main_send, main_recv, mid_send, mid_recv, edge_send, edge_recv, own,
 ):
     i = lax.axis_index("gx")
@@ -94,7 +97,7 @@
     def edge_south():
         return remote(pack.at[0], edge.at[i], edge_send.at[1], edge_recv.at[i], n - 1, before)
 
-    order = [n // 2] + [d for d in range(1, n) if d != n // 2]
+    order = list(range(n - 1, 0, -1))
     for d in order:
         mid_copy(d).start()
 
@@ -116,7 +119,7 @@
         def _():
             remote(pack.at[0], edge.at[k], edge_send.at[0], edge_recv.at[k], i, after).wait_recv()
 
-    first, second = stages(n, m, main, mid, edge, out, fields)
+    first = arrival_stage(n, m, main, mid, edge, fields)
     own_main.wait()
     own_mid.wait()
     edge_arrived(i)
@@ -127,7 +130,6 @@
         edge_arrived(k)
         remote(rows_of(0), main.at[k], main_send.at[d], main_recv.at[k], k, j).wait_recv()
         first(k)
-    second()
 
     for d in order:
         main_copy(d).wait_send()
@@ -142,32 +144,40 @@
         edge_south().wait_send()
 
 
-def face(x0, y0, x1, y1):
+def parts(x0, y0, x1, y1):
     s0, s1 = x0 + y0, x1 + y1
-    return 2.0 * (x0 * y0 * s1 + x1 * y1 * s0) / (s0 * s1)
+    return x0 * y0 * s1 + x1 * y1 * s0, s0 * s1
+
+
+def two_faces(one, two):
+    scale = 2.0 / (one[1] * two[1])
+    return one[0] * two[1] * scale, two[0] * one[1] * scale
 
 
 def middle(one, two):
-    total = 1.0 / (one + two)
-    second = two * total
-    return one * total, second, one * second
-
-
-def with_vertical(sides, k0, k1):
-    vertical = 2.0 * (2.0 * k0 * k1 / (k0 + k1))
-    return (sides + ((k0 + k1) + vertical)) - vertical
-
-
-def stages(n, m, main, mid, edge, out, fields):
+    x, y = one[0] * two[1], two[0] * one[1]
+    total = 1.0 / (x + y)
+    return x * total, y * total, 2.0 * (one[0] * two[0]) * total
+
+
+def verticals(pairs):
+    sums = [x + y for x, y in pairs]
+    low, high = sums[0] * sums[1], sums[2] * sums[3]
+    scale = 4.0 / (low * high)
+    low, high = high * scale, low * scale
+    shares = (sums[1] * low, sums[0] * low, sums[3] * high, sums[2] * high)
+    return [x * y * share for (x, y), share in zip(pairs, shares)]
+
+
+def arrival_stage(n, m, main, mid, edge, fields):
     band = main.shape[2]
     block = main.shape[3]
     half = band // 2
     rows = fields.shape[2]
-    tiles = out.shape[2] // LANES
+    tiles = fields.shape[0] - 1
     per_block = block // (2 * LANES)
     i = lax.axis_index("gx")
     j = lax.axis_index("gy")
-    first_rows = (i == 0) & (j == 0)
     last_rows = (i == n - 1) & (j == m - 1)
 
     taken = 2 * band + 16
@@ -186,16 +196,10 @@
     to = lax.broadcasted_iota(jnp.int32, (2 * LANES, 2 * LANES), 1)
     pick_cols = jnp.where(fine == jnp.where(to < LANES, 2 * to, 2 * (to - LANES) + 1), 1.0, 0.0).astype(jnp.bfloat16)
 
-    lane = lax.broadcasted_iota(jnp.int32, (rows, LANES), 1)
-    sub = lax.broadcasted_iota(jnp.int32, (rows, LANES), 0)
-    bottom = (sub == 0) & first_rows
-    top = (sub == half - 1) & last_rows
+    top = (lax.broadcasted_iota(jnp.int32, (rows, LANES), 0) == half - 1) & last_rows
 
     def up(x):
         return pltpu.roll(x, rows - 1, 0)
-
-    def down(x):
-        return pltpu.roll(x, 1, 0)
 
     def tile_terms(k, part):
         t = k * per_block + part
@@ -213,25 +217,46 @@
         split = jnp.dot(picked, pick_cols, preferred_element_type=jnp.float32)
         a0, c0, a1, c1 = (split[g * rows : (g + 1) * rows, :LANES] for g in range(4))
         b0, d0, b1, d1 = (split[g * rows : (g + 1) * rows, LANES:] for g in range(4))
-        s0, n0, t0 = middle(face(a0, c0, a1, c1), jnp.where(top, c0 + c1, face(c0, up(a0), c1, up(a1))))
-        s1, n1, t1 = middle(face(b0, d0, b1, d1), jnp.where(top, d0 + d1, face(d0, up(b0), d1, up(b1))))
-        h1 = face(a0, b0, a1, b1)
-        g1 = face(c0, d0, c1, d1)
-        side_a = with_vertical(h1, a0, a1)
-        side_b = with_vertical(h1, b0, b1)
-        side_c = with_vertical(g1, c0, c1)
-        side_d = with_vertical(g1, d0, d1)
+        def wall(x0, x1, inner):
+            return jnp.where(top, 0.5 * (x0 + x1), inner[0]), jnp.where(top, 1.0, inner[1])
+
+        s0, n0, t0 = middle(parts(a0, c0, a1, c1), wall(c0, c1, parts(c0, up(a0), c1, up(a1))))
+        s1, n1, t1 = middle(parts(b0, d0, b1, d1), wall(d0, d1, parts(d0, up(b0), d1, up(b1))))
+        h1, g1 = two_faces(parts(a0, b0, a1, b1), parts(c0, d0, c1, d1))
+        pairs = ((a0, a1), (b0, b1), (c0, c1), (d0, d1))
+        side_a, side_b, side_c, side_d = (
+            (x + ((k0 + k1) + v)) - v for x, (k0, k1), v in zip((h1, h1, g1, g1), pairs, verticals(pairs))
+        )
         for at, value in enumerate(
             (a0, a1, c0, c1, s0, n0, b0, b1, d0, d1, t0, s1, n1, t1, h1, g1, side_a, side_b, side_c, side_d)
         ):
             fields[t, at] = value
 
     def first(k):
-        lax.fori_loop(0, per_block, lambda part, carry: (tile_terms(k, part), carry)[1], 0)
+        lax.fori_loop(0, per_block, lambda part, carry: (tile_terms(k, part), carry)[1], 0, unroll=UNROLL)
 
     ones = jnp.ones((rows, LANES), jnp.float32)
     for at in range(6):
         fields[tiles, at] = ones
+
+    return first
+
+
+def stencil_kernel(n, m, half, chunk, fields, out, held, sent):
+    rows = fields.shape[2]
+    tiles = fields.shape[0] - 1
+    i = lax.axis_index("gx")
+    j = lax.axis_index("gy")
+    lane = lax.broadcasted_iota(jnp.int32, (rows, LANES), 1)
+    sub = lax.broadcasted_iota(jnp.int32, (rows, LANES), 0)
+    bottom = (sub == 0) & (i == 0) & (j == 0)
+    top = (sub == half - 1) & (i == n - 1) & (j == m - 1)
+
+    def up(x):
+        return pltpu.roll(x, rows - 1, 0)
+
+    def down(x):
+        return pltpu.roll(x, 1, 0)
 
     def step(t, carry):
         last = (lane == LANES - 1) & (t == tiles - 1)
@@ -251,9 +276,11 @@
         a0, a1, c0, c1, s0, n0, b0, b1, d0, d1 = (fields[t, at] for at in range(10))
         t0, s1, n1, t1, h1, g1, side_a, side_b, side_c, side_d = (fields[t, at] for at in range(10, 20))
         wall_a, wall_b = a0 + a1, b0 + b1
-        h2 = jnp.where(last, wall_b, face(b0, ahead(0), b1, ahead(1)))
-        g2 = jnp.where(last, d0 + d1, face(d0, ahead(2), d1, ahead(3)))
-        left, right, _ = middle(h1, h2)
+        h2, g2 = two_faces(parts(b0, ahead(0), b1, ahead(1)), parts(d0, ahead(2), d1, ahead(3)))
+        h2 = jnp.where(last, wall_b, h2)
+        g2 = jnp.where(last, d0 + d1, g2)
+        total = 1.0 / (h1 + h2)
+        left, right = h1 * total, h2 * total
         left_up = up(left)
         right_up = up(right)
         s0_next = ahead(4)
@@ -302,14 +329,19 @@
         for at, value in enumerate(
             (below(ne_back), below(north), below(north_west), west, centre, east, nw_back, north, north_east)
         ):
-            out[at, :, cols] = value[:half]
+            held[at, :, cols] = value[:half]
         return tuple(rolled)
 
-    def second():
-        zero = jnp.zeros((rows, LANES), jnp.float32)
-        lax.fori_loop(0, tiles, step, (zero,) * 7)
-
-    return first, second
+    def leave(c):
+        cols = pl.ds(c * chunk * LANES, chunk * LANES)
+        return pltpu.make_async_copy(held.at[:, :, cols], out.at[:, :, cols], sent.at[c])
+
+    carry = (jnp.zeros((rows, LANES), jnp.float32),) * 7
+    for c in range(tiles // chunk):
+        carry = lax.fori_loop(c * chunk, (c + 1) * chunk, step, carry, unroll=STEPS)
+        leave(c).start()
+    for c in range(tiles // chunk):
+        leave(c).wait()
 
 
 def shards(n, m, conductivity):
@@ -321,9 +353,10 @@
     vmem = pl.BlockSpec(memory_space=pltpu.VMEM)
     anywhere = pl.BlockSpec(memory_space=pl.ANY)
     dma = pltpu.SemaphoreType.DMA
-    stencil = pl.pallas_call(
+    shape = (tiles + 1, 20, rows, LANES)
+    fields = pl.pallas_call(
         functools.partial(coarse_kernel, n, m),
-        out_shape=jax.ShapeDtypeStruct((9, half, tiles * LANES), jnp.float32),
+        out_shape=jax.ShapeDtypeStruct(shape, jnp.float32),
         in_specs=[anywhere],
         out_specs=vmem,
         scratch_shapes=[
@@ -333,7 +366,6 @@
             pltpu.VMEM((n, planes, 8, local_cols), jnp.bfloat16),
             pltpu.VMEM((n, planes, 8, local_cols), jnp.bfloat16),
             pltpu.VMEM((n + 2, 8, local_cols), jnp.bfloat16),
-            pltpu.VMEM((tiles + 1, 20, rows, LANES), jnp.float32),
             dma((n,)),
             dma((n,)),
             dma((n,)),
@@ -343,10 +375,20 @@
             dma((2 * n + 1,)),
         ],
         compiler_params=pltpu.CompilerParams(
-            collective_id=0, has_side_effects=True, vmem_limit_bytes=24 * 1024 * 1024
+            collective_id=0, has_side_effects=True, vmem_limit_bytes=VMEM_LIMIT
         ),
         name="coarse",
-    )(conductivity)
+    )(pltpu.with_memory_space_constraint(conductivity, pltpu.HBM))
+    chunk = tiles // 4
+    stencil = pl.pallas_call(
+        functools.partial(stencil_kernel, n, m, half, chunk),
+        out_shape=jax.ShapeDtypeStruct((9, half, tiles * LANES), jnp.float32),
+        in_specs=[vmem],
+        out_specs=anywhere,
+        scratch_shapes=[pltpu.VMEM((9, half, tiles * LANES), jnp.float32), dma((4,))],
+        compiler_params=pltpu.CompilerParams(vmem_limit_bytes=VMEM_LIMIT),
+        name="stencil",
+    )(fields)
     return stencil[:, None]
 
 

time: 27 us -> 21.7 us (0.80)
  Pallas kernels: 24.8 us -> 21.6 us
  local copies, waits for them, and re-layouts: 2.06 us -> 0 us
    pallas_call x1, Pallas kernels: 24.8 us -> 19.2 us  [shards(): pl.pallas_call(functools.partial(coarse_kernel, n, m), out_shape=jax.Shap...]
    pallas_call x0 -> x1, Pallas kernels: none -> 2.41 us  [shards(): pl.pallas_call(functools.partial(stencil_kernel, n, m, half, chunk), out_...]
    unnamed x3 -> x0, local copies, waits for them, and re-layouts: 2.06 us -> none
where the time goes in v3:
time: 21.7 us; the launch traced here: 21.6 us
  Pallas kernels  21.6 us (100%)
    pallas_call x1, Pallas kernels, shards(): pl.pallas_call(functools.partial(coarse_kernel, n, m), out_shape=jax.Shap...  19.2 us
    pallas_call x1, Pallas kernels, shards(): pl.pallas_call(functools.partial(stencil_kernel, n, m, half, chunk), out_...  2.41 us

profile of v3, /device:TPU:0, one launch (start us, length us, event | category | flops | bytes accessed | tf_op | source)
XLA Modules:
  0.0 21.6 jit_solution(7350525639638560886)
XLA Ops:
  0.0 19.2 %coarse.1.fields = f32[17,20,24,128]{3,2,1,0:T(8,128)S(1)} custom-call(bf16[2,128,1024]{2,1,0:T(8,128)(2,1)} %cells.1), custom_call_target="tpu_custom_call" | custom-call | tf_op jit(solution)/shard_map/coarse/pallas_call | solution.py:357
  19.2 2.4 %stencil.1 = f32[9,16,2048]{2,1,0:T(8,128)} custom-call(f32[17,20,24,128]{3,2,1,0:T(8,128)S(1)} %coarse.1.fields), custom_call_target="tpu_custom_call" | custom-call | tf_op jit(solution)/shard_map/stencil/pallas_call | solution.py:383

commit v4 on v3

--- a/solution.py
+++ b/solution.py
@@ -56,6 +56,40 @@
         loads.append(pltpu.make_async_copy(cells.at[:, pl.ds(t * band, 8), :], heads.at[t], own.at[2 * t + 1]))
     for load in loads:
         load.start()
+    @pl.when(jnp.logical_not(takes_south | takes_north))
+    def _():
+        edge[...] = jnp.ones(edge.shape, edge.dtype)
+
+    north, south = jnp.where(j < m - 1, 1, 0), jnp.where(j > 0, 1, 0)
+    pl.semaphore_wait(barrier, n - 1 + north + south)
+
+    def remote(src, dst, send, recv, x, y):
+        return pltpu.make_async_remote_copy(
+            src_ref=src, dst_ref=dst, send_sem=send, recv_sem=recv, device_id=(x, y), device_id_type=MESH
+        )
+
+    turn = jnp.where(i < n // 2, 1, n - 1)
+
+    def peer(d):
+        return lax.rem(i + turn * d, n)
+
+    def main_copy(d):
+        t = peer(d)
+        return remote(rows_of(t), main.at[i], main_send.at[d], main_recv.at[i], t, j)
+
+    def mid_copy(d):
+        t = peer(d)
+        return remote(pack.at[t + 1], mid.at[i], mid_send.at[d], mid_recv.at[i], t, j)
+
+    def edge_north():
+        return remote(pack.at[n + 1], edge.at[i], edge_send.at[0], edge_recv.at[i], 0, after)
+
+    def edge_south():
+        return remote(pack.at[0], edge.at[i], edge_send.at[1], edge_recv.at[i], n - 1, before)
+
+    order = list(range(n - 1, 0, -1))
+    for d in order[:2]:
+        main_copy(d).start()
     for load in loads:
         load.wait()
     sub = lax.broadcasted_iota(jnp.int32, (8, cells.shape[2]), 0)
@@ -66,38 +100,6 @@
         rows = jnp.where(sub < 2, low[0], jnp.where(sub < 4, low[1], jnp.where(sub == 4, high[0], high[1])))
         pack[u] = rows.astype(jnp.bfloat16)
 
-    @pl.when(jnp.logical_not(takes_south | takes_north))
-    def _():
-        edge[...] = jnp.ones(edge.shape, edge.dtype)
-
-    north, south = jnp.where(j < m - 1, 1, 0), jnp.where(j > 0, 1, 0)
-    pl.semaphore_wait(barrier, n - 1 + north + south)
-
-    def remote(src, dst, send, recv, x, y):
-        return pltpu.make_async_remote_copy(
-            src_ref=src, dst_ref=dst, send_sem=send, recv_sem=recv, device_id=(x, y), device_id_type=MESH
-        )
-
-    turn = jnp.where(i < n // 2, 1, n - 1)
-
-    def peer(d):
-        return lax.rem(i + turn * d, n)
-
-    def main_copy(d):
-        t = peer(d)
-        return remote(rows_of(t), main.at[i], main_send.at[d], main_recv.at[i], t, j)
-
-    def mid_copy(d):
-        t = peer(d)
-        return remote(pack.at[t + 1], mid.at[i], mid_send.at[d], mid_recv.at[i], t, j)
-
-    def edge_north():
-        return remote(pack.at[n + 1], edge.at[i], edge_send.at[0], edge_recv.at[i], 0, after)
-
-    def edge_south():
-        return remote(pack.at[0], edge.at[i], edge_send.at[1], edge_recv.at[i], n - 1, before)
-
-    order = list(range(n - 1, 0, -1))
     for d in order:
         mid_copy(d).start()
 
@@ -109,7 +111,7 @@
     def _():
         edge_south().start()
 
-    for d in order:
+    for d in order[2:]:
         main_copy(d).start()
     own_mid = pltpu.make_async_copy(pack.at[i + 1], mid.at[i], own.at[1])
     own_mid.start()

time: 21.7 us -> 21.3 us (0.982)
  Pallas kernels: 21.6 us -> 21.1 us
    pallas_call x1, Pallas kernels: 19.2 us -> 18.7 us  [shards(): pl.pallas_call(functools.partial(coarse_kernel, n, m), out_shape=jax.Shap...]
where the time goes in v4:
time: 21.3 us; the launch traced here: 21.1 us
  Pallas kernels  21.1 us (99%)
    pallas_call x1, Pallas kernels, shards(): pl.pallas_call(functools.partial(coarse_kernel, n, m), out_shape=jax.Shap...  18.7 us
    pallas_call x1, Pallas kernels, shards(): pl.pallas_call(functools.partial(stencil_kernel, n, m, half, chunk), out_...  2.41 us

profile of v4, /device:TPU:0, one launch (start us, length us, event | category | flops | bytes accessed | tf_op | source)
XLA Modules:
  0.0 21.1 jit_solution(4867318147412847160)
XLA Ops:
  0.0 18.7 %coarse.1.fields = f32[17,20,24,128]{3,2,1,0:T(8,128)S(1)} custom-call(bf16[2,128,1024]{2,1,0:T(8,128)(2,1)} %cells.1), custom_call_target="tpu_custom_call" | custom-call | tf_op jit(solution)/shard_map/coarse/pallas_call | solution.py:359
  18.7 2.4 %stencil.1 = f32[9,16,2048]{2,1,0:T(8,128)} custom-call(f32[17,20,24,128]{3,2,1,0:T(8,128)S(1)} %coarse.1.fields), custom_call_target="tpu_custom_call" | custom-call | tf_op jit(solution)/shard_map/stencil/pallas_call | solution.py:385

commit v5 on v4

--- a/solution.py
+++ b/solution.py
@@ -68,10 +68,11 @@
             src_ref=src, dst_ref=dst, send_sem=send, recv_sem=recv, device_id=(x, y), device_id_type=MESH
         )
 
-    turn = jnp.where(i < n // 2, 1, n - 1)
+    near = jnp.where(i < n // 2, i, n - 1 - i)
 
     def peer(d):
-        return lax.rem(i + turn * d, n)
+        t = jnp.where(d > near, d, d - 1)
+        return jnp.where(i < n // 2, t, n - 1 - t)
 
     def main_copy(d):
         t = peer(d)

time: 21.3 us -> 23.9 us (1.12)
  Pallas kernels: 21.1 us -> 23.7 us
    pallas_call x1, Pallas kernels: 18.7 us -> 21.3 us  [shards(): pl.pallas_call(functools.partial(coarse_kernel, n, m), out_shape=jax.Shap...]
where the time goes in v5:
time: 23.9 us; the launch traced here: 23.8 us
  Pallas kernels  23.7 us (99%)
    pallas_call x1, Pallas kernels, shards(): pl.pallas_call(functools.partial(coarse_kernel, n, m), out_shape=jax.Shap...  21.3 us
    pallas_call x1, Pallas kernels, shards(): pl.pallas_call(functools.partial(stencil_kernel, n, m, half, chunk), out_...  2.41 us

profile of v5, /device:TPU:0, one launch (start us, length us, event | category | flops | bytes accessed | tf_op | source)
XLA Modules:
  0.0 23.8 jit_solution(1746575462532980185)
XLA Ops:
  0.0 21.3 %coarse.1.fields = f32[17,20,24,128]{3,2,1,0:T(8,128)S(1)} custom-call(bf16[2,128,1024]{2,1,0:T(8,128)(2,1)} %cells.1), custom_call_target="tpu_custom_call" | custom-call | tf_op jit(solution)/shard_map/coarse/pallas_call | solution.py:360
  21.3 2.4 %stencil.1 = f32[9,16,2048]{2,1,0:T(8,128)} custom-call(f32[17,20,24,128]{3,2,1,0:T(8,128)S(1)} %coarse.1.fields), custom_call_target="tpu_custom_call" | custom-call | tf_op jit(solution)/shard_map/stencil/pallas_call | solution.py:386
